TPU v7x, 256 devices: a whole 4x4x8 slice. The times are simulated.
256 devices in a mesh: dp: 2 (over x_hi), tm: 16 (over z, x_lo), mp: 8 (over y, core).
Axes of the slice: x: 4 (x_hi: 2, x_lo: 2; x = x_hi * 2 + x_lo), y: 4, z: 8, core: 2. Of those that a mesh axis runs over, the one named last changes fastest.
Arguments:
- features: bfloat16 [128, 576, 1024], P(('dp', 'tm'), 'mp'), parts along dimension 0, may hold values from -6 to 6
- queries: bfloat16 [8192, 1024], P(('dp', 'tm')), parts along dimension 0, may hold values from -6 to 6
- anchor_frame: int32 [8192], P(('dp', 'tm')), parts along dimension 0, may hold values from 0 to 63, as said below
- anchor_patch: int32 [8192], P(('dp', 'tm')), parts along dimension 0, may hold values from 0 to 575
- time_offset: float32 [8192, 8, 4], P(('dp', 'tm')), parts along dimension 0, may hold values from -1.99 to 1.99
- space_offset: float32 [2, 8192, 8, 4], P(None, ('dp', 'tm')), parts along dimension 1, may hold values from -3 to 3
- value_weight: bfloat16 [1024, 1024], replicated, may hold values from -0.1875 to 0.1875
- point_weight: bfloat16 [1024, 32], replicated, may hold values from -0.1875 to 0.1875
- point_bias: float32 [32], replicated, may hold values from -6 to 260
- output_weight: bfloat16 [1024, 1024], P('mp'), may hold values from -0.1875 to 0.1875
- project_weight: bfloat16 [1024, 3584], P(None, 'mp'), may hold values from -2 to 2
- norm_gain: float32 [3584], P('mp'), may hold values from 0.1 to 1.9
- query_weight: bfloat16 [3584, 3072], P(None, 'mp'), may hold values from -0.09375 to 0.09375
- query_bias: float32 [3072], P('mp'), may hold values from -6 to 40
- cache_weight: bfloat16 [3584, 1024], P(None, 'mp'), may hold values from -0.09375 to 0.09375
- cache_bias: float32 [1024], P('mp'), may hold values from -6 to 40
Outputs:
- attention: bfloat16 [8192, 3072], P(('dp', 'tm'), 'mp'), parts along dimension 0
- key_value: bfloat16 [8192, 1024], P(('dp', 'tm'), 'mp'), parts along dimension 0
There are 2 independent parts, one for each index of `dp`. A program takes and returns all parts, laid end to end along the dimension named above; an argument that names none is the same for every part. Nothing has to cross between parts.
Inputs may be any that keep to these rules, and one draw needn't show every extreme that they name: `anchor_frame`: the anchor frame of query q lies among the 4 frames that begin at (q // 256) * 4.
All inputs are finite; a program needn't handle non-finite values.
Results may differ from a plain program's by a relative error of at most 0.04.
Values may be sent and summed in bfloat16 or wider, within the bound.
No kernel may reach another device: no remote copies, remote signals or barrier semaphores. Data moves between devices by JAX's collectives and lax.ppermute only.
A program may use at most 64 MiB of HBM per device.

v0:
```python
import jax
import jax.numpy as jnp
from jax import lax
from jax.sharding import Mesh
from jax.sharding import PartitionSpec as P

AH = 8
POINTS = 4
GRID = 24
KVH = 4
HD = 128
GROUP = 7
MP = ("mp_0", "mp_1")
rope_base = 1000000.0
epsilon = 1e-06
masked = -1e30


def with_halo(block, sides, width):
    for axis, dim in sides:
        count = lax.axis_size(axis)
        forward = [(i, i + 1) for i in range(count - 1)]
        backward = [(target, source) for source, target in forward]
        low = lax.ppermute(
            lax.slice_in_dim(block, block.shape[dim] - width, None, axis=dim), axis, forward
        )
        high = lax.ppermute(lax.slice_in_dim(block, 0, width, axis=dim), axis, backward)
        block = jnp.concatenate([low, block, high], axis=dim)
    return block


def gathered_total(x, axis):
    return lax.all_gather(x, axis).sum(0)


def sent_to_all(x, axis):
    copies = jnp.broadcast_to(x, (lax.axis_size(axis), *x.shape))
    return lax.all_to_all(copies, axis, split_axis=0, concat_axis=0, tiled=True)


def of_everyone(x, axis):
    return sent_to_all(x, axis).sum(axis=0)


def in_order(parts, dim):
    lengths = list(parts.shape[1:])
    lengths[dim] *= parts.shape[0]
    return jnp.moveaxis(parts, 0, dim).reshape(lengths)


def stacked_from(x, axes, sequence):
    parts = x
    for k in sequence:
        parts = lax.all_gather(parts, axes[k])
    done = sequence[::-1]
    back = [done.index(k) for k in range(len(axes))]
    parts = parts.transpose(*back, *range(len(axes), parts.ndim))
    return parts.reshape(-1, *x.shape)


def gather_axes(x, axes, sequence, dim):
    return in_order(stacked_from(x, axes, sequence), dim)


def gather_directly(x, axis, dim):
    return in_order(sent_to_all(x, axis), dim)


def sent_together(arrays, axis, dim, along):
    both = jnp.concatenate(arrays, axis=along)
    out, at, outs = (lax.all_gather(both, axis, axis=dim, tiled=True), 0, [])
    for a in arrays:
        outs.append(lax.slice_in_dim(out, at, at + a.shape[along], axis=along))
        at += a.shape[along]
    return tuple(outs)


def rotate(vectors, positions):
    half_width = vectors.shape[-1] // 2
    frequency = rope_base ** (-2.0 * jnp.arange(half_width, dtype=jnp.float32) / vectors.shape[-1])
    angles = positions.astype(jnp.float32)[:, None] * frequency[None, :]
    cosine = jnp.cos(angles)[:, None, :]
    sine_part = jnp.sin(angles)[:, None, :]
    first_half = vectors[..., :half_width]
    second_half = vectors[..., half_width:]
    return jnp.concatenate(
        [
            first_half * cosine - second_half * sine_part,
            second_half * cosine + first_half * sine_part,
        ],
        axis=-1,
    )


def trilinear_corners(frame_pos, row_pos, column_pos, weight, frame_total, side):
    floor_frame = jnp.floor(frame_pos)
    floor_row = jnp.floor(row_pos)
    floor_column = jnp.floor(column_pos)
    frame_part = frame_pos - floor_frame
    row_part = row_pos - floor_row
    column_part = column_pos - floor_column
    frame_start = floor_frame.astype(jnp.int32)
    row_start = floor_row.astype(jnp.int32)
    column_start = floor_column.astype(jnp.int32)
    listing = []
    for frame_step in (0, 1):
        for row_step in (0, 1):
            for column_step in (0, 1):
                frame_cell = frame_start + frame_step
                row_cell = row_start + row_step
                column_cell = column_start + column_step
                portion = weight * (frame_part if frame_step else 1.0 - frame_part)
                portion = portion * (row_part if row_step else 1.0 - row_part)
                portion = portion * (column_part if column_step else 1.0 - column_part)
                inside = (
                    (frame_cell >= 0)
                    & (frame_cell < frame_total)
                    & (row_cell >= 0)
                    & (row_cell < side)
                )
                inside = inside & (column_cell >= 0) & (column_cell < side)
                portion = jnp.where(inside, portion, 0.0)
                patch_id = jnp.clip(row_cell, 0, side - 1) * side + jnp.clip(
                    column_cell, 0, side - 1
                )
                listing.append((frame_cell, patch_id, portion))
    return listing


def make_attend(query_turned, positions, head_map, scaling):

    def attend(state_in, members, first_row):
        key_rows, value_rows = members
        length = key_rows.shape[0]
        block_len = 512
        block_count = length // block_len
        key_blocks = key_rows.reshape(block_count, block_len, -1, HD)[:, :, head_map, :]
        value_blocks = value_rows.reshape(block_count, block_len, -1, HD)[:, :, head_map, :]
        block_starts = jnp.arange(block_count, dtype=jnp.int32) * block_len

        def advance(running, inputs):
            peak_score, denominator, numerator = running
            key_block, value_block, block_start = inputs
            scores = (
                jnp.einsum(
                    "qhd,nhd->hqn", query_turned, key_block, preferred_element_type=jnp.float32
                )
                * scaling
            )
            key_pos = block_start + jnp.arange(block_len, dtype=jnp.int32)
            allowed = key_pos[None, None, :] <= positions[None, :, None]
            scores = jnp.where(allowed, scores, masked)
            new_peak = jnp.maximum(peak_score, jnp.max(scores, axis=-1))
            weights = jnp.where(allowed, jnp.exp(scores - new_peak[..., None]), 0.0)
            rescale = jnp.exp(peak_score - new_peak)
            denominator = denominator * rescale + jnp.sum(weights, axis=-1)
            numerator = numerator * rescale[..., None] + jnp.einsum(
                "hqn,nhd->hqd",
                weights.astype(jnp.bfloat16),
                value_block,
                preferred_element_type=jnp.float32,
            )
            return ((new_peak, denominator, numerator), None)

        result, unused = lax.scan(advance, state_in, (key_blocks, value_blocks, block_starts))
        return result

    return attend


def local(
    features,
    queries,
    anchor_frame,
    anchor_patch,
    time_offset,
    space_offset,
    value_weight,
    point_weight,
    point_bias,
    output_weight,
    project_weight,
    norm_gain,
    query_weight,
    query_bias,
    cache_weight,
    cache_bias,
):
    groups = lax.axis_size(MP)
    group_index = lax.axis_index(MP)
    frame_index = lax.axis_index("tm")
    frames_here, patches_here, feature_width = features.shape
    rows_here = queries.shape[0]
    frame_total = frames_here * lax.axis_size("tm")
    patch_total = GRID * GRID
    head_width = feature_width // AH
    heads_here = AH // groups
    first_frame = frame_index * frames_here - 2
    projected = jnp.dot(
        features.reshape(frames_here * patches_here, feature_width),
        value_weight,
        preferred_element_type=jnp.float32,
    )
    projected = projected.astype(jnp.bfloat16).reshape(frames_here, patches_here, feature_width)
    logits = jnp.dot(queries, point_weight, preferred_element_type=jnp.float32) + point_bias
    point_share = jax.nn.softmax(logits.reshape(rows_here, AH, POINTS), axis=-1)
    frame_pos = anchor_frame.astype(jnp.float32)[:, None, None] + time_offset
    row_pos = (anchor_patch // GRID).astype(jnp.float32)[:, None, None] + space_offset[0]
    column_pos = (anchor_patch % GRID).astype(jnp.float32)[:, None, None] + space_offset[1]

    def own_slice(array):
        return lax.dynamic_slice_in_dim(array, group_index * heads_here, heads_here, 1)

    by_head = lax.all_to_all(projected, MP, split_axis=2, concat_axis=1, tiled=True)
    padded = with_halo(by_head, (("tm", 0),), 2)
    lookup = padded.reshape(-1, heads_here, head_width)
    head_lane = jnp.arange(heads_here, dtype=jnp.int32)[None, :, None]
    running = jnp.zeros((rows_here, heads_here, head_width), jnp.float32)
    for frame_cell, patch_id, portion in trilinear_corners(
        own_slice(frame_pos),
        own_slice(row_pos),
        own_slice(column_pos),
        own_slice(point_share),
        frame_total,
        GRID,
    ):
        local_frame = jnp.clip(frame_cell - first_frame, 0, frames_here + 3)
        picked = lookup[local_frame * patch_total + patch_id, head_lane]
        running = running + jnp.sum(portion[..., None] * picked.astype(jnp.float32), axis=2)
    sampled = running.reshape(rows_here, heads_here * head_width).astype(jnp.bfloat16)
    head_terms = jnp.dot(sampled, output_weight, preferred_element_type=jnp.float32)
    head_mix = gathered_total(head_terms, MP)
    abstract = (queries.astype(jnp.float32) + head_mix).astype(jnp.bfloat16)
    visual = jnp.dot(abstract, project_weight, preferred_element_type=jnp.float32)
    squares = of_everyone(jnp.sum(visual * visual, axis=1), MP)
    model_width = query_weight.shape[0]
    normed = (visual * lax.rsqrt(squares / model_width + epsilon)[:, None] * norm_gain).astype(
        jnp.bfloat16
    )
    shard_piece = gather_axes(normed, MP, (0, 1), 1)
    query_sum = jnp.dot(shard_piece, query_weight, preferred_element_type=jnp.float32)
    cache_sum = jnp.dot(shard_piece, cache_weight, preferred_element_type=jnp.float32)
    positions = frame_index * rows_here + jnp.arange(rows_here, dtype=jnp.int32)
    query_heads = query_weight.shape[1] // HD
    query_turned = rotate(
        (query_sum + query_bias).reshape(rows_here, query_heads, HD), positions
    ).astype(jnp.bfloat16)
    cache_heads = cache_weight.shape[1] // HD
    cache_state = (cache_sum + cache_bias).reshape(rows_here, cache_heads, HD)
    is_key = group_index * cache_heads + jnp.arange(cache_heads, dtype=jnp.int32) < KVH
    cache_state = jnp.where(is_key[None, :, None], rotate(cache_state, positions), cache_state)
    key_value = cache_state.reshape(rows_here, cache_heads * HD).astype(jnp.bfloat16)
    cache_all = gather_directly(key_value, MP, 1)
    key_rows = cache_all[:, : KVH * HD]
    value_rows = cache_all[:, KVH * HD :]
    own_heads = (group_index * query_heads + jnp.arange(query_heads, dtype=jnp.int32)) // GROUP
    scaling = HD ** (-0.5)
    initial = (
        jnp.full((query_heads, rows_here), masked, jnp.float32),
        jnp.zeros((query_heads, rows_here), jnp.float32),
        jnp.zeros((query_heads, rows_here, HD), jnp.float32),
    )
    span_heads = min(KVH, (query_heads - 1) // GROUP + 2)
    lowest = jnp.minimum(group_index * query_heads // GROUP, KVH - span_heads)
    key_rows = lax.dynamic_slice_in_dim(key_rows, lowest * HD, span_heads * HD, 1)
    value_rows = lax.dynamic_slice_in_dim(value_rows, lowest * HD, span_heads * HD, 1)
    attend = make_attend(query_turned, positions, own_heads - lowest, scaling)
    peak_score, denominator, numerator = attend(
        initial, sent_together((key_rows, value_rows), "tm", 0, 1), jnp.int32(0)
    )
    attention = (
        (numerator / denominator[..., None])
        .transpose(1, 0, 2)
        .reshape(rows_here, query_heads * HD)
        .astype(jnp.bfloat16)
    )
    return (attention, key_value)


def solution(mesh):
    finer = Mesh(
        mesh.devices.reshape(mesh.shape["dp"], mesh.shape["tm"], 4, 2), ("dp", "tm", "mp_0", "mp_1")
    )
    placed = (
        P(("dp", "tm"), MP, None),
        P(("dp", "tm"), None),
        P(("dp", "tm")),
        P(("dp", "tm")),
        P(("dp", "tm"), None, None),
        P(None, ("dp", "tm"), None, None),
        P(),
        P(),
        P(),
        P(MP, None),
        P(None, MP),
        P(MP),
        P(None, MP),
        P(MP),
        P(None, MP),
        P(MP),
    )
    return jax.shard_map(
        local,
        mesh=finer,
        in_specs=placed,
        out_specs=(P(("dp", "tm"), MP), P(("dp", "tm"), MP)),
        check_vma=False,
    )
```

profile of v0, /device:TPU:2, one launch (start us, length us, event | category | flops | bytes accessed | tf_op | source)
XLA Modules:
  0.0 492.8 jit_solution(13112427165565141134)
XLA Ops:
  7.2 3.5 convolution_convert_fusion
  10.7 2.4 copy.159
  13.1 4.6 all-to-all-start
  19.2 14.6 %all-to-all-done = bf16[4,72,1024]{1,0,2:T(4,128)(2,1)} async-done(((bf16[4,72,1024]{1,0,2:T(4,128)(2,1)}), bf16[4,72,1024]{1,0,2:T(4,128)(2,1)}, u32[]{:S(2)}, u32[]{:S(2)}) %all-to-all-start) | async-done | bytes 589856 | tf_op jit(solution)/shard_map/all_to_all | solution.py:214
  33.8 3.5 fusion.75
  37.2 1.9 copy.160
  39.2 3.8 collective-permute-start
  44.0 2.9 collective-permute-start.1
  56.4 2.2 pad_maximum_fusion
  58.6 16.0 %gather_fusion = bf16[1024,128]{1,0:T(8,128)(2,1)} fusion(bf16[4608,1,128]{2,0,1:T(8,128)(2,1)} %bitcast.166, s32[1024]{0:T(1024)S(1)} %reshape.427), kind=kCustom, calls=%fused_computation | custom fusion | bytes 532480 | tf_op jit(solution)/shard_map/gather | solution.py:228
  74.6 16.0 %gather_fusion.1 = bf16[1024,128]{1,0:T(8,128)(2,1)} fusion(bf16[4608,1,128]{2,0,1:T(8,128)(2,1)} %bitcast.167, s32[1024]{0:T(1024)S(1)} %reshape.435), kind=kCustom, calls=%fused_computation.1 | custom fusion | bytes 532480 | tf_op jit(solution)/shard_map/gather | solution.py:228
  90.6 16.0 %gather_fusion.2 = bf16[1024,128]{1,0:T(8,128)(2,1)} fusion(bf16[4608,1,128]{2,0,1:T(8,128)(2,1)} %bitcast.168, s32[1024]{0:T(1024)S(1)} %reshape.443), kind=kCustom, calls=%fused_computation.2 | custom fusion | bytes 532480 | tf_op jit(solution)/shard_map/gather | solution.py:228
  106.6 16.0 %gather_fusion.3 = bf16[1024,128]{1,0:T(8,128)(2,1)} fusion(bf16[4608,1,128]{2,0,1:T(8,128)(2,1)} %bitcast.169, s32[1024]{0:T(1024)S(1)} %reshape.451), kind=kCustom, calls=%fused_computation.3 | custom fusion | bytes 532480 | tf_op jit(solution)/shard_map/gather | solution.py:228
  122.7 15.9 %gather_fusion.4 = bf16[1024,128]{1,0:T(8,128)(2,1)} fusion(bf16[4608,1,128]{2,0,1:T(8,128)(2,1)} %bitcast.170, s32[1024]{0:T(1024)S(1)} %reshape.459), kind=kCustom, calls=%fused_computation.4 | custom fusion | bytes 532480 | tf_op jit(solution)/shard_map/gather | solution.py:228
  138.6 16.0 %gather_fusion.5 = bf16[1024,128]{1,0:T(8,128)(2,1)} fusion(bf16[4608,1,128]{2,0,1:T(8,128)(2,1)} %bitcast.171, s32[1024]{0:T(1024)S(1)} %reshape.467), kind=kCustom, calls=%fused_computation.5 | custom fusion | bytes 532480 | tf_op jit(solution)/shard_map/gather | solution.py:228
  154.6 11.4 %gather_fusion.6 = bf16[1024,128]{1,0:T(8,128)(2,1)S(1)} fusion(bf16[4608,1,128]{2,0,1:T(8,128)(2,1)} %bitcast.172, s32[1024]{0:T(1024)S(1)} %reshape.475), kind=kCustom, calls=%fused_computation.6 | custom fusion | bytes 532480 | tf_op jit(solution)/shard_map/gather | solution.py:228
  165.9 11.4 %gather_fusion.7 = bf16[1024,128]{1,0:T(8,128)(2,1)S(1)} fusion(bf16[4608,1,128]{2,0,1:T(8,128)(2,1)} %bitcast.173, s32[1024]{0:T(1024)S(1)} %reshape.483), kind=kCustom, calls=%fused_computation.7 | custom fusion | bytes 532480 | tf_op jit(solution)/shard_map/gather | solution.py:228
  186.6 55.3 %all-gather.9.cloned.1.call-done = f32[2048,1024]{1,0:T(8,128)} async-done(((f32[256,1024]{1,0:T(8,128)}), f32[2048,1024]{1,0:T(8,128)}) %all-gather.9.cloned.1.call-update) | async-done | bytes 8388624 | tf_op jit(solution)/shard_map/all_gather | solution.py:33
  241.9 5.5 %reduce_sum.126 = f32[256,1024]{1,0:T(8,128)} reduce(f32[8,256,1024]{2,1,0:T(8,128)} %bitcast.176, f32[]{:T(128)} %constant.44.clone.1), dimensions={0}, to_apply=%region_10.11 | reduce | flops 1835008 | bytes 9437188 | tf_op jit(solution)/shard_map/reduce_sum | solution.py:33
  247.4 2.7 multiply_reduce_fusion
  250.1 8.3 %all_to_all.29 = f32[8,1,256]{2,1,0:T(1,128)S(1)} all-to-all(f32[8,1,256]{2,1,0:T(1,128)S(1)} %broadcast_in_dim.123), channel_id=1, replica_groups=mesh['dp'=2,'tm'=16,'mp_0'=4,'mp_1'=2] {'mp_0','mp_1'}, dimensions={0} | all-to-all | bytes 16384 | tf_op jit(solution)/shard_map/all_to_all | solution.py:38
  259.6 14.3 %all-gather.1 = bf16[1024,448]{0,1:T(8,128)(2,1)S(1)} all-gather(bf16[256,448]{0,1:T(8,128)(2,1)S(1)} %multiply_convert_fusion), channel_id=3, replica_groups=mesh['dp'=2,'tm'=16,'mp_0'=4,'mp_1'=2] {'mp_0'}, dimensions={0}, use_global_device_ids=true | all-gather | bytes 1146880 | tf_op jit(solution)/shard_map/all_gather | solution.py:54
  274.9 15.4 %all-gather.11.cloned.1.call-done = bf16[8,256,448]{1,2,0:T(8,128)(2,1)} async-done(((bf16[4,256,448]{1,2,0:T(8,128)(2,1)}), bf16[8,256,448]{1,2,0:T(8,128)(2,1)}) %all-gather.11.cloned.1.call-update) | async-done | bytes 1835024 | tf_op jit(solution)/shard_map/all_gather | solution.py:54
  295.0 4.4 all-to-all-start.2
  299.5 10.3 %all-to-all-done.2 = bf16[8,256,128]{1,2,0:T(8,128)(2,1)S(1)} async-done(((bf16[8,256,128]{1,2,0:T(8,128)(2,1)}), bf16[8,256,128]{1,2,0:T(8,128)(2,1)S(1)}, u32[]{:S(2)}, u32[]{:S(2)}) %all-to-all-start.2) | async-done | bytes 524320 | tf_op jit(solution)/shard_map/all_to_all | solution.py:38
  311.7 3.4 convolution_add_fusion.1
  316.5 113.7 %all-gather.7.cloned.1.call-done = bf16[4096,512]{0,1:T(8,128)(2,1)} async-done(((bf16[256,512]{0,1:T(8,128)(2,1)}), bf16[4096,512]{0,1:T(8,128)(2,1)}) %all-gather.7.cloned.1.call-update) | async-done | bytes 4194320 | tf_op jit(solution)/shard_map/all_gather | solution.py:71
  430.2 2.7 fusion.74
  435.5 2.0 copy.181
  437.5 2.5 gather_fusion.9
  440.0 4.1 gather_fusion.8
  444.1 40.3 %while.15 = (s32[]{:T(128)}, f32[3,256]{1,0:T(4,128)S(1)}, f32[3,256]{1,0:T(4,128)S(1)}, f32[3,256,128]{2,1,0:T(8,128)S(1)}, s32[8]{0:T(128)S(1)}, /*index=5*/bf...) while((s32[]{:T(128)}, f32[3,256]{1,0:T(4,128)S(1)}, ...), condition=%wide.region_16.17_spmd.clone, body=%wide.region_13.16_spmd.clone.sunk | while | flops 205296128 | bytes 7068813 | solution.py:165
  (224 shorter events, 75.0 us)
Async XLA Ops:
  7.2 304.5 %copy-start = (bf16[3584,384]{1,0:T(8,128)(2,1)S(1)}, bf16[3584,384]{1,0:T(8,128)(2,1)}, u32[]{:S(2)}) copy-start(bf16[3584,384]{1,0:T(8,128)(2,1)} %param.30) | copy-start | bytes 8257540
  10.7 7.1 %copy-start.2 = (bf16[256,1024]{1,0:T(8,128)(2,1)S(1)}, bf16[256,1024]{1,0:T(8,128)(2,1)}, u32[]{:S(2)}) copy-start(bf16[256,1024]{1,0:T(8,128)(2,1)} %param.19) | copy-start | bytes 1572868
  10.7 7.1 %copy-start.13 = (bf16[1024,32]{0,1:T(8,128)(2,1)S(1)}, bf16[1024,32]{0,1:T(8,128)(2,1)}, u32[]{:S(2)}) copy-start(bf16[1024,32]{0,1:T(8,128)(2,1)} %param.25) | copy-start | bytes 196612
  10.7 7.1 %copy-start.17 = (f32[32]{0:T(128)S(1)}, f32[32]{0:T(128)}, u32[]{:S(2)}) copy-start(f32[32]{0:T(128)} %param.26) | copy-start | bytes 388
  13.1 5.1 %copy-start.12 = (f32[2,256,8,4]{1,3,2,0:T(4,128)S(1)}, f32[2,256,8,4]{1,3,2,0:T(4,128)}, u32[]{:S(2)}) copy-start(f32[2,256,8,4]{1,3,2,0:T(4,128)} %param.23) | copy-start | bytes 196612
  13.1 5.1 %copy-start.15 = (s32[256]{0:T(256)S(1)}, s32[256]{0:T(256)}, u32[]{:S(2)}) copy-start(s32[256]{0:T(256)} %param.21) | copy-start | bytes 3076
  13.1 5.1 %copy-start.16 = (s32[256]{0:T(256)S(1)}, s32[256]{0:T(256)}, u32[]{:S(2)}) copy-start(s32[256]{0:T(256)} %param.20) | copy-start | bytes 3076
  13.1 20.7 %all-to-all-start = ((bf16[4,72,1024]{1,0,2:T(4,128)(2,1)}), bf16[4,72,1024]{1,0,2:T(4,128)(2,1)}, u32[]{:S(2)}, u32[]{:S(2)}) async-start(bf16[4,72,1024]{1,0,2:T(4,128)(2,1)} %copy.159), calls=%async_computation | async-start | bytes 2097152 | tf_op jit(solution)/shard_map/all_to_all | solution.py:214
  17.7 224.1 %all-gather.9.cloned.1.call-start = ((), (), s32[]{:S(2)}) async-start(), calls=%async_computation.4 | async-start | bytes 9437184 | tf_op jit(solution)/shard_map/all_gather | solution.py:33
  39.2 17.2 %collective-permute-start = (bf16[2,576,128]{2,1,0:T(8,128)(2,1)}, bf16[2,576,128]{2,1,0:T(8,128)(2,1)}, u32[]{:S(2)}, u32[]{:S(2)}) collective-permute-start(bf16[2,576,128]{2,1,0:T(8,128)(2,1)} %bitcast.200), channel_id=1, source_target_pairs={{0,8},{8,16},{16,24},{24,32},{32,40},{40,48},{48,56},{56,64},{64,7... | collective-permute-start | bytes 884744 | tf_op jit(solution)/shard_map/ppermute | solution.py:24
  44.0 12.4 %collective-permute-start.1 = (bf16[2,576,128]{2,1,0:T(8,128)(2,1)}, bf16[2,576,128]{2,1,0:T(8,128)(2,1)}, u32[]{:S(2)}, u32[]{:S(2)}) collective-permute-start(bf16[2,576,128]{2,1,0:T(8,128)(2,1)} %bitcast.201), channel_id=1, source_target_pairs={{8,0},{16,8},{24,16},{32,24},{40,32},{48,40},{56,48},{64,56},{72,6... | collective-permute-start | bytes 884744 | tf_op jit(solution)/shard_map/ppermute | solution.py:27
  177.4 5.8 %copy-start.6 = (bf16[1024,128]{1,0:T(8,128)(2,1)S(1)}, bf16[1024,128]{1,0:T(8,128)(2,1)}, u32[]{:S(2)}) copy-start(bf16[1024,128]{1,0:T(8,128)(2,1)} %gather_fusion.4) | copy-start | bytes 786436
  177.4 5.8 %copy-start.7 = (f32[256,4]{1,0:T(8,128)S(1)}, f32[256,4]{1,0:T(8,128)}, u32[]{:S(2)}) copy-start(f32[256,4]{1,0:T(8,128)} %copy.170) | copy-start | bytes 12292
  177.4 6.2 %copy-start.5 = (bf16[1024,128]{1,0:T(8,128)(2,1)S(1)}, bf16[1024,128]{1,0:T(8,128)(2,1)}, u32[]{:S(2)}) copy-start(bf16[1024,128]{1,0:T(8,128)(2,1)} %gather_fusion.5) | copy-start | bytes 786436
  177.4 6.2 %copy-start.8 = (f32[256,4]{1,0:T(8,128)S(1)}, f32[256,4]{1,0:T(8,128)}, u32[]{:S(2)}) copy-start(f32[256,4]{1,0:T(8,128)} %copy.172) | copy-start | bytes 12292
  177.4 6.6 %copy-start.9 = (f32[256,4]{1,0:T(8,128)S(1)}, f32[256,4]{1,0:T(8,128)}, u32[]{:S(2)}) copy-start(f32[256,4]{1,0:T(8,128)} %copy.174) | copy-start | bytes 12292
  177.4 7.0 %copy-start.10 = (f32[256,4]{1,0:T(8,128)S(1)}, f32[256,4]{1,0:T(8,128)}, u32[]{:S(2)}) copy-start(f32[256,4]{1,0:T(8,128)} %copy.176) | copy-start | bytes 12292
  178.9 6.0 %copy-start.11 = (bf16[128,1024]{1,0:T(8,128)(2,1)S(1)}, bf16[128,1024]{1,0:T(8,128)(2,1)}, u32[]{:S(2)}) copy-start(bf16[128,1024]{1,0:T(8,128)(2,1)} %param.27) | copy-start | bytes 786436
  186.3 104.0 %all-gather.11.cloned.1.call-start = ((), (), s32[]{:S(2)}) async-start(), calls=%async_computation.5 | async-start | bytes 2752512 | tf_op jit(solution)/shard_map/all_gather | solution.py:54
  241.8 5.5 %copy-start.3 = (bf16[256,1024]{1,0:T(8,128)(2,1)S(1)}, bf16[256,1024]{1,0:T(8,128)(2,1)}, u32[]{:S(2)}) copy-start(bf16[256,1024]{1,0:T(8,128)(2,1)} %param.19) | copy-start | bytes 1572868
  247.3 11.1 %copy-start.14 = (f32[448]{0:T(512)S(1)}, f32[448]{0:T(512)}, u32[]{:S(2)}) copy-start(f32[448]{0:T(512)} %param.29) | copy-start | bytes 5380
  290.3 3.0 copy-start.18
  290.3 3.0 copy-start.20
  292.0 1.3 copy-start.4
  295.0 16.7 %copy-start.19 = (f32[384]{0:T(512)S(1)}, f32[384]{0:T(512)}, u32[]{:S(2)}) copy-start(f32[384]{0:T(512)} %param.31) | copy-start | bytes 4612
  295.0 14.8 %all-to-all-start.2 = ((bf16[8,256,128]{1,2,0:T(8,128)(2,1)}), bf16[8,256,128]{1,2,0:T(8,128)(2,1)S(1)}, u32[]{:S(2)}, u32[]{:S(2)}) async-start(bf16[8,256,128]{1,2,0:T(8,128)(2,1)} %broadcast_in_dim.124), calls=%async_computation.2 | async-start | bytes 1048576 | tf_op jit(solution)/shard_map/all_to_all | solution.py:38
  299.4 130.9 %all-gather.7.cloned.1.call-start = ((), (), s32[]{:S(2)}) async-start(), calls=%async_computation.3 | async-start | bytes 4456448 | tf_op jit(solution)/shard_map/all_gather | solution.py:71
  484.4 1.9 copy-start.1
Sparse Core Ops, SparseCore 0:
  186.4 55.3 all-gather.8
  275.0 15.2 all-gather.10
  310.7 119.5 all-gather.6
where the time goes:
time: 495 us; the launch traced here: 493 us
  waiting for transfers between devices  209 us (42%)
  local copies, waits for them, and re-layouts  165 us (33%)
  matrix products  36.9 us (7%)
  other arithmetic  28 us (6%)
  blocking collectives  22.6 us (5%)
  starting transfers between devices  16.1 us (3%)
  between operations  14.6 us (3%)
    gather x8, local copies, waits for them, and re-layouts, local(): picked = lookup[local_frame * patch_total + patch_id, head_lane]  119 us
    all_gather x1, waiting for transfers between devices, sent_together(): out, at, outs = (lax.all_gather(both, axis, axis=dim, tiled=True), 0, [])  114 us
    all_gather x1, waiting for transfers between devices, gathered_total(): return lax.all_gather(x, axis).sum(0)  55.3 us
    all_gather x1, waiting for transfers between devices, stacked_from(): parts = lax.all_gather(parts, axes[k])  15.4 us
    all_to_all x1, waiting for transfers between devices, local(): lax.all_to_all(projected, MP, split_axis=2, concat_axis=1, tiled=True)  14.6 us
    all_gather x1, blocking collectives, stacked_from(): parts = lax.all_gather(parts, axes[k])  14.3 us
    dot_general x8, matrix products, advance(): jnp.einsum('hqn,nhd->hqd', weights.astype(jnp.bfloat16), value_block, pre...  13.1 us
    dot_general x8, matrix products, advance(): jnp.einsum('qhd,nhd->hqn', query_turned, key_block, preferred_element_typ...  11.9 us
  transfers between devices with their start and end apart: 7, of which 5 were waited for; matrix products, arithmetic and copies ran while one was open for 4% of the time, Pallas kernels for 0%

commit v1 on v0

--- a/solution.py
+++ b/solution.py
@@ -211,7 +211,9 @@
     def own_slice(array):
         return lax.dynamic_slice_in_dim(array, group_index * heads_here, heads_here, 1)
 
-    by_head = lax.all_to_all(projected, MP, split_axis=2, concat_axis=1, tiled=True)
+    by_head = jnp.concatenate(
+        lax.all_to_all(jnp.stack(jnp.split(projected, lax.axis_size(MP), axis=2)), MP, 0, 0), axis=1
+    )
     padded = with_halo(by_head, (("tm", 0),), 2)
     lookup = padded.reshape(-1, heads_here, head_width)
     head_lane = jnp.arange(heads_here, dtype=jnp.int32)[None, :, None]

time: 495 us -> 516 us (1.042)
  other arithmetic: 28 us -> 41.6 us
  matrix products: 36.9 us -> 48.9 us
  waiting for transfers between devices: 209 us -> 203 us
    reduce_sum x8, other arithmetic: 2.48 us -> 13.7 us  [advance(): denominator = denominator * rescale + jnp.sum(weights, axis=-1)]
    dot_general x8, matrix products: 11.9 us -> 21 us  [advance(): jnp.einsum('qhd,nhd->hqn', query_turned, key_block, preferred_element_typ...]
    unnamed x47 -> x54, local copies, waits for them, and re-layouts: 5.67 us -> 10.4 us
  transfers between devices with their start and end apart: 7 -> 7, of which waited for: 5 -> 6; matrix products, arithmetic and copies ran while one was open for 4% -> 4% of each run, Pallas kernels for 0% -> 0%
where the time goes in v1:
time: 516 us; the launch traced here: 513 us
  waiting for transfers between devices  203 us (39%)
  local copies, waits for them, and re-layouts  166 us (32%)
  matrix products  48.9 us (9%)
  other arithmetic  41.6 us (8%)
  blocking collectives  22.6 us (4%)
  starting transfers between devices  15.7 us (3%)
  between operations  14.6 us (3%)
    gather x8, local copies, waits for them, and re-layouts, local(): picked = lookup[local_frame * patch_total + patch_id, head_lane]  119 us
    all_gather x1, waiting for transfers between devices, sent_together(): out, at, outs = (lax.all_gather(both, axis, axis=dim, tiled=True), 0, [])  110 us
    all_gather x1, waiting for transfers between devices, gathered_total(): return lax.all_gather(x, axis).sum(0)  55.5 us
    dot_general x8, matrix products, advance(): jnp.einsum('qhd,nhd->hqn', query_turned, key_block, preferred_element_typ...  21 us
    dot_general x8, matrix products, advance(): jnp.einsum('hqn,nhd->hqd', weights.astype(jnp.bfloat16), value_block, pre...  16.9 us
    all_gather x1, waiting for transfers between devices, stacked_from(): parts = lax.all_gather(parts, axes[k])  15.4 us
    all_gather x1, blocking collectives, stacked_from(): parts = lax.all_gather(parts, axes[k])  14.3 us
    reduce_sum x8, other arithmetic, advance(): denominator = denominator * rescale + jnp.sum(weights, axis=-1)  13.7 us
  transfers between devices with their start and end apart: 7, of which 6 were waited for; matrix products, arithmetic and copies ran while one was open for 4% of the time, Pallas kernels for 0%

profile of v1, /device:TPU:2, one launch (start us, length us, event | category | flops | bytes accessed | tf_op | source)
XLA Modules:
  0.0 513.3 jit_solution(10665661853371768038)
XLA Ops:
  7.2 2.7 convolution_convert_fusion
  15.2 4.5 all-to-all-start
  21.1 9.6 %all-to-all-done = bf16[8,4,72,128]{3,2,1,0:T(8,128)(2,1)} async-done(((bf16[8,4,72,128]{3,2,1,0:T(8,128)(2,1)}), bf16[8,4,72,128]{3,2,1,0:T(8,128)(2,1)}, u32[]{:S(2)}, u32[]{:S(2)}) %all-to-all-start) | async-done | bytes 589856 | tf_op jit(solution)/shard_map/all_to_all | solution.py:215
  32.8 3.8 collective-permute-start
  36.6 2.7 collective-permute-start.1
  52.1 16.0 %gather_fusion = bf16[1024,128]{1,0:T(8,128)(2,1)} fusion(bf16[4608,1,128]{2,0,1:T(8,128)(2,1)} %bitcast.198, s32[1024]{0:T(1024)S(1)} %reshape.435), kind=kCustom, calls=%fused_computation | custom fusion | bytes 532480 | tf_op jit(solution)/shard_map/gather | solution.py:230
  68.1 16.0 %gather_fusion.1 = bf16[1024,128]{1,0:T(8,128)(2,1)} fusion(bf16[4608,1,128]{2,0,1:T(8,128)(2,1)} %bitcast.199, s32[1024]{0:T(1024)S(1)} %reshape.443), kind=kCustom, calls=%fused_computation.1 | custom fusion | bytes 532480 | tf_op jit(solution)/shard_map/gather | solution.py:230
  84.0 16.0 %gather_fusion.2 = bf16[1024,128]{1,0:T(8,128)(2,1)} fusion(bf16[4608,1,128]{2,0,1:T(8,128)(2,1)} %bitcast.200, s32[1024]{0:T(1024)S(1)} %reshape.451), kind=kCustom, calls=%fused_computation.2 | custom fusion | bytes 532480 | tf_op jit(solution)/shard_map/gather | solution.py:230
  100.1 16.0 %gather_fusion.3 = bf16[1024,128]{1,0:T(8,128)(2,1)} fusion(bf16[4608,1,128]{2,0,1:T(8,128)(2,1)} %bitcast.201, s32[1024]{0:T(1024)S(1)} %reshape.459), kind=kCustom, calls=%fused_computation.3 | custom fusion | bytes 532480 | tf_op jit(solution)/shard_map/gather | solution.py:230
  116.1 15.9 %gather_fusion.4 = bf16[1024,128]{1,0:T(8,128)(2,1)} fusion(bf16[4608,1,128]{2,0,1:T(8,128)(2,1)} %bitcast.202, s32[1024]{0:T(1024)S(1)} %reshape.467), kind=kCustom, calls=%fused_computation.4 | custom fusion | bytes 532480 | tf_op jit(solution)/shard_map/gather | solution.py:230
  132.0 16.0 %gather_fusion.5 = bf16[1024,128]{1,0:T(8,128)(2,1)} fusion(bf16[4608,1,128]{2,0,1:T(8,128)(2,1)} %bitcast.203, s32[1024]{0:T(1024)S(1)} %reshape.475), kind=kCustom, calls=%fused_computation.5 | custom fusion | bytes 532480 | tf_op jit(solution)/shard_map/gather | solution.py:230
  148.0 11.4 %gather_fusion.6 = bf16[1024,128]{1,0:T(8,128)(2,1)S(1)} fusion(bf16[4608,1,128]{2,0,1:T(8,128)(2,1)} %bitcast.204, s32[1024]{0:T(1024)S(1)} %reshape.483), kind=kCustom, calls=%fused_computation.6 | custom fusion | bytes 532480 | tf_op jit(solution)/shard_map/gather | solution.py:230
  159.4 11.4 %gather_fusion.7 = bf16[1024,128]{1,0:T(8,128)(2,1)S(1)} fusion(bf16[4608,1,128]{2,0,1:T(8,128)(2,1)} %bitcast.205, s32[1024]{0:T(1024)S(1)} %reshape.491), kind=kCustom, calls=%fused_computation.7 | custom fusion | bytes 532480 | tf_op jit(solution)/shard_map/gather | solution.py:230
  180.0 55.5 %all-gather.9.cloned.1.call-done = f32[2048,1024]{1,0:T(8,128)} async-done(((f32[256,1024]{1,0:T(8,128)}), f32[2048,1024]{1,0:T(8,128)}) %all-gather.9.cloned.1.call-update) | async-done | bytes 8388624 | tf_op jit(solution)/shard_map/all_gather | solution.py:33
  235.5 5.5 %reduce_sum.126 = f32[256,1024]{1,0:T(8,128)} reduce(f32[8,256,1024]{2,1,0:T(8,128)} %bitcast.208, f32[]{:T(128)} %constant.44.clone.1), dimensions={0}, to_apply=%region_10.11 | reduce | flops 1835008 | bytes 9437188 | tf_op jit(solution)/shard_map/reduce_sum | solution.py:33
  241.0 2.7 multiply_reduce_fusion
  243.7 8.3 %all_to_all.16 = f32[8,1,256]{2,1,0:T(1,128)S(1)} all-to-all(f32[8,1,256]{2,1,0:T(1,128)S(1)} %broadcast_in_dim.123), channel_id=1, replica_groups=mesh['dp'=2,'tm'=16,'mp_0'=4,'mp_1'=2] {'mp_0','mp_1'}, dimensions={0} | all-to-all | bytes 16384 | tf_op jit(solution)/shard_map/all_to_all | solution.py:38
  253.2 14.3 %all-gather.1 = bf16[1024,448]{0,1:T(8,128)(2,1)S(1)} all-gather(bf16[256,448]{0,1:T(8,128)(2,1)S(1)} %multiply_convert_fusion), channel_id=3, replica_groups=mesh['dp'=2,'tm'=16,'mp_0'=4,'mp_1'=2] {'mp_0'}, dimensions={0}, use_global_device_ids=true | all-gather | bytes 1146880 | tf_op jit(solution)/shard_map/all_gather | solution.py:54
  268.5 15.4 %all-gather.11.cloned.1.call-done = bf16[8,256,448]{1,2,0:T(8,128)(2,1)} async-done(((bf16[4,256,448]{1,2,0:T(8,128)(2,1)}), bf16[8,256,448]{1,2,0:T(8,128)(2,1)}) %all-gather.11.cloned.1.call-update) | async-done | bytes 1835024 | tf_op jit(solution)/shard_map/all_gather | solution.py:54
  288.6 4.4 all-to-all-start.2
  293.1 10.3 %all-to-all-done.2 = bf16[8,256,128]{1,2,0:T(8,128)(2,1)S(1)} async-done(((bf16[8,256,128]{1,2,0:T(8,128)(2,1)}), bf16[8,256,128]{1,2,0:T(8,128)(2,1)S(1)}, u32[]{:S(2)}, u32[]{:S(2)}) %all-to-all-start.2) | async-done | bytes 524320 | tf_op jit(solution)/shard_map/all_to_all | solution.py:38
  305.3 3.4 convolution_add_fusion.1
  313.5 110.3 %all-gather.7.cloned.1.call-done = bf16[4096,512]{0,1:T(8,128)(2,1)} async-done(((bf16[256,512]{0,1:T(8,128)(2,1)}), bf16[4096,512]{0,1:T(8,128)(2,1)}) %all-gather.7.cloned.1.call-update) | async-done | bytes 4194320 | tf_op jit(solution)/shard_map/all_gather | solution.py:71
  423.9 2.7 fusion.82
  432.5 4.1 gather_fusion.9
  436.6 4.1 gather_fusion.8
  440.7 63.3 %while.15 = (s32[]{:T(128)}, f32[3,256]{1,0:T(4,128)S(1)}, f32[3,256]{1,0:T(4,128)S(1)}, f32[3,256,128]{2,1,0:T(8,128)S(1)}, s32[8]{0:T(128)S(1)}, /*index=5*/bf...) while((s32[]{:T(128)}, f32[3,256]{1,0:T(4,128)S(1)}, ...), condition=%wide.region_16.17_spmd.clone, body=%wide.region_13.16_spmd.clone.sunk | while | flops 205296128 | bytes 7068813 | solution.py:165
  450.0 2.6 fusion.106
  457.9 2.6 fusion.106
  465.9 2.6 fusion.106
  489.6 2.6 fusion.106
  497.5 2.6 fusion.106
  (229 shorter events, 102.1 us)
Async XLA Ops:
  7.2 298.2 %copy-start = (bf16[3584,384]{1,0:T(8,128)(2,1)S(1)}, bf16[3584,384]{1,0:T(8,128)(2,1)}, u32[]{:S(2)}) copy-start(bf16[3584,384]{1,0:T(8,128)(2,1)} %param.30) | copy-start | bytes 8257540
  9.9 9.8 %copy-start.1 = (bf16[256,1024]{1,0:T(8,128)(2,1)S(1)}, bf16[256,1024]{1,0:T(8,128)(2,1)}, u32[]{:S(2)}) copy-start(bf16[256,1024]{1,0:T(8,128)(2,1)} %param.19) | copy-start | bytes 1572868
  9.9 9.8 %copy-start.13 = (bf16[1024,32]{0,1:T(8,128)(2,1)S(1)}, bf16[1024,32]{0,1:T(8,128)(2,1)}, u32[]{:S(2)}) copy-start(bf16[1024,32]{0,1:T(8,128)(2,1)} %param.25) | copy-start | bytes 196612
  9.9 9.8 %copy-start.17 = (f32[32]{0:T(128)S(1)}, f32[32]{0:T(128)}, u32[]{:S(2)}) copy-start(f32[32]{0:T(128)} %param.26) | copy-start | bytes 388
  9.9 10.1 %copy-start.12 = (f32[2,256,8,4]{1,3,2,0:T(4,128)S(1)}, f32[2,256,8,4]{1,3,2,0:T(4,128)}, u32[]{:S(2)}) copy-start(f32[2,256,8,4]{1,3,2,0:T(4,128)} %param.23) | copy-start | bytes 196612
  9.9 10.2 %copy-start.15 = (s32[256]{0:T(256)S(1)}, s32[256]{0:T(256)}, u32[]{:S(2)}) copy-start(s32[256]{0:T(256)} %param.21) | copy-start | bytes 3076
  9.9 10.2 %copy-start.16 = (s32[256]{0:T(256)S(1)}, s32[256]{0:T(256)}, u32[]{:S(2)}) copy-start(s32[256]{0:T(256)} %param.20) | copy-start | bytes 3076
  15.2 15.6 %all-to-all-start = ((bf16[8,4,72,128]{3,2,1,0:T(8,128)(2,1)}), bf16[8,4,72,128]{3,2,1,0:T(8,128)(2,1)}, u32[]{:S(2)}, u32[]{:S(2)}) async-start(bf16[8,4,72,128]{3,2,1,0:T(8,128)(2,1)} %fusion.30), calls=%async_computation | async-start | bytes 1179648 | tf_op jit(solution)/shard_map/all_to_all | solution.py:215
  19.6 215.9 %all-gather.9.cloned.1.call-start = ((), (), s32[]{:S(2)}) async-start(), calls=%async_computation.4 | async-start | bytes 9437184 | tf_op jit(solution)/shard_map/all_gather | solution.py:33
  32.8 17.1 %collective-permute-start = (bf16[2,576,128]{2,1,0:T(8,128)(2,1)}, bf16[2,576,128]{2,1,0:T(8,128)(2,1)}, u32[]{:S(2)}, u32[]{:S(2)}) collective-permute-start(bf16[2,576,128]{2,1,0:T(8,128)(2,1)} %bitcast.14), channel_id=1, source_target_pairs={{0,8},{8,16},{16,24},{24,32},{32,40},{40,48},{48,56},{56,64},{64,7... | collective-permute-start | bytes 884744 | tf_op jit(solution)/shard_map/ppermute | solution.py:24
  36.6 13.3 %collective-permute-start.1 = (bf16[2,576,128]{2,1,0:T(8,128)(2,1)}, bf16[2,576,128]{2,1,0:T(8,128)(2,1)}, u32[]{:S(2)}, u32[]{:S(2)}) collective-permute-start(bf16[2,576,128]{2,1,0:T(8,128)(2,1)} %bitcast.16), channel_id=1, source_target_pairs={{8,0},{16,8},{24,16},{32,24},{40,32},{48,40},{56,48},{64,56},{72,6... | collective-permute-start | bytes 884744 | tf_op jit(solution)/shard_map/ppermute | solution.py:27
  159.4 11.5 %copy-start.6 = (f32[256,4]{1,0:T(8,128)S(1)}, f32[256,4]{1,0:T(8,128)}, u32[]{:S(2)}) copy-start(f32[256,4]{1,0:T(8,128)} %copy.157) | copy-start | bytes 12292
  170.8 5.8 %copy-start.5 = (bf16[1024,128]{1,0:T(8,128)(2,1)S(1)}, bf16[1024,128]{1,0:T(8,128)(2,1)}, u32[]{:S(2)}) copy-start(bf16[1024,128]{1,0:T(8,128)(2,1)} %gather_fusion.4) | copy-start | bytes 786436
  170.8 5.8 %copy-start.7 = (f32[256,4]{1,0:T(8,128)S(1)}, f32[256,4]{1,0:T(8,128)}, u32[]{:S(2)}) copy-start(f32[256,4]{1,0:T(8,128)} %copy.166) | copy-start | bytes 12292
  170.8 6.2 %copy-start.4 = (bf16[1024,128]{1,0:T(8,128)(2,1)S(1)}, bf16[1024,128]{1,0:T(8,128)(2,1)}, u32[]{:S(2)}) copy-start(bf16[1024,128]{1,0:T(8,128)(2,1)} %gather_fusion.5) | copy-start | bytes 786436
  170.8 6.2 %copy-start.8 = (f32[256,4]{1,0:T(8,128)S(1)}, f32[256,4]{1,0:T(8,128)}, u32[]{:S(2)}) copy-start(f32[256,4]{1,0:T(8,128)} %copy.168) | copy-start | bytes 12292
  170.9 6.6 %copy-start.9 = (f32[256,4]{1,0:T(8,128)S(1)}, f32[256,4]{1,0:T(8,128)}, u32[]{:S(2)}) copy-start(f32[256,4]{1,0:T(8,128)} %copy.170) | copy-start | bytes 12292
  170.9 7.0 %copy-start.10 = (f32[256,4]{1,0:T(8,128)S(1)}, f32[256,4]{1,0:T(8,128)}, u32[]{:S(2)}) copy-start(f32[256,4]{1,0:T(8,128)} %copy.172) | copy-start | bytes 12292
  172.3 6.0 %copy-start.11 = (bf16[128,1024]{1,0:T(8,128)(2,1)S(1)}, bf16[128,1024]{1,0:T(8,128)(2,1)}, u32[]{:S(2)}) copy-start(bf16[128,1024]{1,0:T(8,128)(2,1)} %param.27) | copy-start | bytes 786436
  179.7 104.2 %all-gather.11.cloned.1.call-start = ((), (), s32[]{:S(2)}) async-start(), calls=%async_computation.5 | async-start | bytes 2752512 | tf_op jit(solution)/shard_map/all_gather | solution.py:54
  235.5 5.5 %copy-start.2 = (bf16[256,1024]{1,0:T(8,128)(2,1)S(1)}, bf16[256,1024]{1,0:T(8,128)(2,1)}, u32[]{:S(2)}) copy-start(bf16[256,1024]{1,0:T(8,128)(2,1)} %param.19) | copy-start | bytes 1572868
  241.0 11.1 %copy-start.14 = (f32[448]{0:T(512)S(1)}, f32[448]{0:T(512)}, u32[]{:S(2)}) copy-start(f32[448]{0:T(512)} %param.29) | copy-start | bytes 5380
  283.9 3.0 copy-start.18
  283.9 3.0 copy-start.20
  285.6 1.3 copy-start.3
  288.6 16.7 %copy-start.19 = (f32[384]{0:T(512)S(1)}, f32[384]{0:T(512)}, u32[]{:S(2)}) copy-start(f32[384]{0:T(512)} %param.31) | copy-start | bytes 4612
  288.6 14.8 %all-to-all-start.2 = ((bf16[8,256,128]{1,2,0:T(8,128)(2,1)}), bf16[8,256,128]{1,2,0:T(8,128)(2,1)S(1)}, u32[]{:S(2)}, u32[]{:S(2)}) async-start(bf16[8,256,128]{1,2,0:T(8,128)(2,1)} %broadcast_in_dim.124), calls=%async_computation.2 | async-start | bytes 1048576 | tf_op jit(solution)/shard_map/all_to_all | solution.py:38
  293.0 130.9 %all-gather.7.cloned.1.call-start = ((), (), s32[]{:S(2)}) async-start(), calls=%async_computation.3 | async-start | bytes 4456448 | tf_op jit(solution)/shard_map/all_gather | solution.py:71
Sparse Core Ops, SparseCore 0:
  179.8 55.5 all-gather.8
  268.6 15.2 all-gather.10
  304.3 119.5 all-gather.6
